TPU v7x, 256 devices: a whole 4x4x8 slice. The times are simulated.
256 devices in a mesh: space: 8 (over y, core), tm: 32 (over x, z).
Axes of the slice: x: 4, y: 4, z: 8, core: 2. Of those that a mesh axis runs over, the one named last changes fastest.
Arguments:
- snapshots: bfloat16 [8192, 32768], P('space', 'tm'), may hold values from -6 to 6
- basis: bfloat16 [8192, 64], P('space'), may hold values from -0.0625 to 0.0625
- lengths: int32 [16], replicated, may hold values from 1540 to 2048
Outputs:
- gram_matrix: float32 [2144, 2144], P('space')
- right_sides: float32 [2144, 64], P('space')
Inputs may be any that keep to these rules, and one draw needn't show every extreme that they name: lengths[k] snapshots of trajectory k are recorded; later positions of its slot of 2048 are padding.
All inputs are finite; a program needn't handle non-finite values.
Results may differ from a plain program's by a relative error of at most 0.0003.
Values sent between devices are 32-bit elements; how exact they have to be, the bound alone decides.
No kernel may reach another device: no remote copies, remote signals or barrier semaphores. Data moves between devices by JAX's collectives and lax.ppermute only.
A program may use at most 64 MiB of HBM per device.

v0:
```python
import jax
import jax.numpy as jnp
import numpy as np
from jax import lax
from jax.sharding import PartitionSpec as P

FEAT = 2144
EXACT = lax.Precision.HIGHEST


def extended(cells, sides, width):
    for axis, dim in sides:
        count = lax.axis_size(axis)
        ends = count - 1
        head = lax.slice_in_dim(cells, 0, width, axis=dim)
        tail = lax.slice_in_dim(cells, cells.shape[dim] - width, cells.shape[dim], axis=dim)
        cells = jnp.concatenate(
            [
                lax.ppermute(tail, axis, [(i, (i + 1) % count) for i in range(ends)]),
                cells,
                lax.ppermute(head, axis, [((i + 1) % count, i) for i in range(ends)]),
            ],
            axis=dim,
        )
    return cells


def selectors(modes_count):
    firsts, seconds = np.triu_indices(modes_count)
    modes = np.arange(modes_count)[:, None]
    pick_first = jnp.asarray((modes == firsts[None, :]).astype(np.float32))
    pick_second = jnp.asarray((modes == seconds[None, :]).astype(np.float32))
    return (pick_first, pick_second)


def features(block_rows):
    pick_first, pick_second = selectors(block_rows.shape[1])
    first = jnp.dot(block_rows, pick_first, precision=EXACT, preferred_element_type=jnp.float32)
    second = jnp.dot(block_rows, pick_second, precision=EXACT, preferred_element_type=jnp.float32)
    return jnp.concatenate([block_rows, first * second], axis=1)


def outer_rows(left_part, right_part):
    return jnp.einsum(
        "tf,tg->fg", left_part, right_part, precision=EXACT, preferred_element_type=jnp.float32
    )


def energy_sum(energy_part):
    return lax.psum(energy_part, ("space", "tm"))


def stencil(padded, width):
    return (
        padded[:, :width]
        - 8.0 * padded[:, 1 : width + 1]
        + 8.0 * padded[:, 3 : width + 3]
        - padded[:, 4:]
    ) / 12.0


def shards(snapshots, basis, lengths):
    partial_value = jnp.einsum("cr,ct->rt", basis, snapshots, preferred_element_type=jnp.float32)
    horizon = partial_value.shape[1]
    time_index = lax.axis_index("tm")
    cell_index = lax.axis_index("space")
    padded = extended(partial_value, (("tm", 1),), 2)
    change_part = stencil(padded, horizon)
    states, change = (
        lax.psum_scatter(partial_value, "space", scatter_dimension=1, tiled=True),
        lax.psum_scatter(change_part, "space", scatter_dimension=1, tiled=True),
    )
    share = states.shape[1]
    slot_width = 2 * horizon
    traj_count = lengths.shape[0]
    shifted = (
        time_index * horizon
        + cell_index * share
        + jnp.arange(share, dtype=jnp.int32)
        + horizon // 2
    )
    offsets = shifted % slot_width
    owners = shifted // slot_width % traj_count
    match = owners[:, None] == jnp.arange(traj_count, dtype=jnp.int32)[None, :]
    limits = jnp.sum(jnp.where(match, lengths[None, :], 0), axis=1)
    living = ((offsets >= 2) & (offsets <= limits - 3)).astype(jnp.float32)
    samples = jnp.sum(lengths - 4).astype(jnp.float32)
    masked = states * living[None, :]
    dmasked = change * living[None, :]
    energy_part = jnp.sum(masked * masked, axis=1)
    row_count = FEAT // lax.axis_size("space")
    scales = jnp.sqrt(energy_sum(energy_part) / samples + 1e-06)
    masked = masked / scales[:, None]
    dmasked = dmasked / scales[:, None]
    whole_states, whole_change = (
        lax.all_gather(masked, "space", axis=1, tiled=True),
        lax.all_gather(dmasked, "space", axis=1, tiled=True),
    )
    design = features(whole_states.T)
    picked = lax.dynamic_slice_in_dim(design, cell_index * row_count, row_count, 1)
    gram_part = outer_rows(picked, design)
    side_part = outer_rows(picked, whole_change.T)
    gram_part, side_part = lax.psum((gram_part, side_part), "tm")
    return (gram_part / samples, side_part / samples)


def solution(mesh):
    return jax.shard_map(
        shards,
        mesh=mesh,
        in_specs=(P("space", "tm"), P("space", None), P()),
        out_specs=(P("space", None), P("space", None)),
        check_vma=False,
    )
```

profile of v0, /device:TPU:8, one launch (start us, length us, event | category | flops | bytes accessed | tf_op | source)
XLA Modules:
  0.0 340.6 jit_solution(10435550340036665465)
XLA Ops:
  7.2 1.5 copy-done
  8.8 2.1 fusion.14
  10.9 0.9 fusion.13
  11.8 3.8 %collective-permute-start = (f32[64,2]{1,0:T(8,128)S(1)}, f32[64,2]{1,0:T(8,128)S(1)}, u32[]{:S(2)}, u32[]{:S(2)}) collective-permute-start(f32[64,2]{1,0:T(8,128)S(1)} %get-tuple-element.4), channel_id=1, source_target_pairs={{0,1},{1,2},{2,3},{3,4},{4,5},{5,6},{6,7},{7,8},{8,9},{9,10},{10,1... | collective-permute-start | bytes 1544 | tf_op jit(solution)/shard_map/ppermute | solution.py:19
  15.6 1.3 collective-permute-start.1
  17.0 0.1 select_reduce_fusion
  17.0 0.6 add_reduce_fusion
  18.3 3.1 collective-permute-done.1
  21.4 2.4 fusion.7
  23.8 0.0 all-reduce.3.cloned.1.call-start
  23.9 20.7 %reduce-scatter.3.cloned.1.call-done = f32[64,128]{1,0:T(8,128)} async-done(((f32[64,1024]{1,0:T(8,128)}), f32[64,128]{1,0:T(8,128)}) %reduce-scatter.3.cloned.1.call-update) | async-done | bytes 32784 | tf_op jit(solution)/shard_map/reduce_scatter | solution.py:70
  44.5 0.9 multiply_reduce_fusion
  45.4 77.0 %psum.21 = f32[64]{0:T(128)S(1)} all-reduce(f32[64]{0:T(128)S(1)} %multiply_reduce_fusion), channel_id=1, replica_groups=mesh['space'=8,'tm'=32] {'space','tm'}, use_global_device_ids=true, to_apply=%region_3.4 | all-reduce | flops 64 | bytes 512 | tf_op jit(solution)/shard_map/psum | solution.py:50
  122.4 0.9 multiply_divide_fusion
  123.3 12.9 %all_gather.6 = f32[64,1024]{1,0:T(8,128)S(1)} all-gather(f32[64,128]{1,0:T(8,128)S(1)} %get-tuple-element.7), channel_id=1, replica_groups=mesh['space'=8,'tm'=32] {'space'}, dimensions={1}, use_global_device_ids=true | all-gather | bytes 294912 | tf_op jit(solution)/shard_map/all_gather | solution.py:96
  136.2 7.0 %fusion.15 = f32[1024,2080]{0,1:T(8,128)S(1)} fusion(f32[64,1024]{1,0:T(8,128)S(1)} %all_gather.6, f32[64,2080]{1,0:T(8,128)S(1)} %copy-done.2), kind=kOutput, calls=%fused_computation.44 | convolution fusion | flops 1635778560 | bytes 9314304 | tf_op jit(solution)/shard_map/dot_general | solution.py:38
  143.2 7.3 %convolution_multiply_fusion = f32[1024,2080]{0,1:T(8,128)S(1)} fusion(f32[1024,2080]{0,1:T(8,128)S(1)} %fusion.15, f32[64,1024]{1,0:T(8,128)S(1)} %all_gather.6, f32[64,2080]{1,0:T(8,128)S(1)} %copy-done.1), kind=kOutput, calls=%fused_computation.5 | convolution fusion | flops 1637908480 | bytes 17833984 | tf_op jit(solution)/shard_map/dot_general | solution.py:39
  150.5 0.2 fusion.2
  150.7 9.9 %fusion = f32[268,2144]{1,0:T(8,128)} fusion(f32[1024,268]{0,1:T(8,128)S(1)} %fusion.2, f32[1024,64]{0,1:T(8,128)S(1)} %bitcast.11, f32[1024,2080]{0,1:T(8,128)S(1)} %convolution_multiply_fusion), kind=kOutput, calls=%fused_computation.2 | convolution fusion | flops 7062781952 | bytes 12177920 | tf_op jit(solution)/shard_map/tf,tg->fg/dot_general | solution.py:44
  160.6 12.9 %all_gather.7 = f32[64,1024]{1,0:T(8,128)S(1)} all-gather(f32[64,128]{1,0:T(8,128)S(1)} %get-tuple-element.6), channel_id=1, replica_groups=mesh['space'=8,'tm'=32] {'space'}, dimensions={1}, use_global_device_ids=true | all-gather | bytes 294912 | tf_op jit(solution)/shard_map/all_gather | solution.py:97
  173.5 1.9 fusion.16
  175.4 154.8 %all-reduce.3.cloned.1.call-done = (f32[268,2144]{1,0:T(8,128)}, f32[268,64]{0,1:T(8,128)}) async-done(((f32[268,2144]{1,0:T(8,128)}, f32[268,64]{0,1:T(8,128)}), (f32[268,2144]{1,0:T(8,128)}, f32[268,64]{0,1:T(8,128)})) %all-reduce.3.cloned.1.call-update) | async-done | bytes 2366992 | tf_op jit(solution)/shard_map/psum | solution.py:103
  330.2 3.3 broadcast_divide_fusion
  333.5 0.7 broadcast_divide_fusion.1
  (19 shorter events, 0.2 us)
Async XLA Ops:
  7.2 1.6 copy-start
  7.2 129.0 %copy-start.2 = (f32[64,2080]{1,0:T(8,128)S(1)}, f32[64,2080]{1,0:T(8,128)}, u32[]{:S(2)}) copy-start(f32[64,2080]{1,0:T(8,128)} %constant.80.clone) | copy-start | bytes 1597444
  7.2 9.8 %copy-start.4 = (s32[16]{0:T(128)S(1)}, s32[16]{0:T(128)}, u32[]{:S(2)}) copy-start(s32[16]{0:T(128)} %param.7) | copy-start | bytes 196
  7.2 37.3 %reduce-scatter.3.cloned.1.call-start = ((), (), s32[]{:S(2)}) async-start(), calls=%async_computation.2 | async-start | bytes 294912 | tf_op jit(solution)/shard_map/reduce_scatter | solution.py:70
  10.9 111.5 %reduce-scatter.5.cloned.1.call-start = ((), (), s32[]{:S(2)}) async-start(), calls=%async_computation.3 | async-start | bytes 294912 | tf_op jit(solution)/shard_map/reduce_scatter | solution.py:71
  11.8 6.5 %collective-permute-start = (f32[64,2]{1,0:T(8,128)S(1)}, f32[64,2]{1,0:T(8,128)S(1)}, u32[]{:S(2)}, u32[]{:S(2)}) collective-permute-start(f32[64,2]{1,0:T(8,128)S(1)} %get-tuple-element.4), channel_id=1, source_target_pairs={{0,1},{1,2},{2,3},{3,4},{4,5},{5,6},{6,7},{7,8},{8,9},{9,10},{10,1... | collective-permute-start | bytes 1544 | tf_op jit(solution)/shard_map/ppermute | solution.py:19
  15.6 5.8 %collective-permute-start.1 = (f32[64,2]{1,0:T(8,128)S(1)}, f32[64,2]{1,0:T(8,128)S(1)}, u32[]{:S(2)}, u32[]{:S(2)}) collective-permute-start(f32[64,2]{1,0:T(8,128)S(1)} %get-tuple-element.5), channel_id=1, source_target_pairs={{1,0},{2,1},{3,2},{4,3},{5,4},{6,5},{7,6},{8,7},{9,8},{10,9},{11,1... | collective-permute-start | bytes 1544 | tf_op jit(solution)/shard_map/ppermute | solution.py:21
  23.8 306.4 %all-reduce.3.cloned.1.call-start = ((), (), s32[]{:S(2)}) async-start(), calls=%async_computation.4 | async-start | bytes 4931584 | tf_op jit(solution)/shard_map/psum | solution.py:103
  136.2 7.0 %copy-start.1 = (f32[64,2080]{1,0:T(8,128)S(1)}, f32[64,2080]{1,0:T(8,128)}, u32[]{:S(2)}) copy-start(f32[64,2080]{1,0:T(8,128)} %constant.81.clone) | copy-start | bytes 1597444
  330.2 3.3 copy-start.3
Sparse Core Ops, SparseCore 0:
  11.1 33.4 reduce-scatter.2
  47.0 32.4 reduce-scatter.4
  175.6 154.5 all-reduce.2
where the time goes:
time: 341 us
  waiting for transfers between devices  179 us (52%)
  blocking collectives  103 us (30%)
  matrix products  28.1 us (8%)
  between operations  14.5 us (4%)
  other arithmetic  8.98 us (3%)
  starting transfers between devices  5.23 us (2%)
    psum x1, waiting for transfers between devices, shards(): gram_part, side_part = lax.psum((gram_part, side_part), 'tm')  155 us
    psum x1, blocking collectives, energy_sum(): return lax.psum(energy_part, ('space', 'tm'))  77 us
    reduce_scatter x1, waiting for transfers between devices, shards(): lax.psum_scatter(partial_value, 'space', scatter_dimension=1, tiled=True)  20.7 us
    all_gather x1, blocking collectives, shards(): lax.all_gather(dmasked, 'space', axis=1, tiled=True)  12.9 us
    all_gather x1, blocking collectives, shards(): lax.all_gather(masked, 'space', axis=1, tiled=True)  12.9 us
    dot_general x2, matrix products, outer_rows(): jnp.einsum('tf,tg->fg', left_part, right_part, precision=EXACT, preferred...  11.8 us
    dot_general x1, matrix products, features(): jnp.dot(block_rows, pick_second, precision=EXACT, preferred_element_type=...  7.29 us
    dot_general x1, matrix products, features(): jnp.dot(block_rows, pick_first, precision=EXACT, preferred_element_type=j...  6.96 us
  transfers between devices with their start and end apart: 5, of which 3 were waited for; matrix products, arithmetic and copies ran while one was open for 1% of the time, Pallas kernels for 0%

commit v1 on v0

--- a/solution.py
+++ b/solution.py
@@ -47,7 +47,7 @@
 
 
 def energy_sum(energy_part):
-    return lax.psum(energy_part, ("space", "tm"))
+    return jnp.sum(lax.all_gather(energy_part, ("space", "tm")), 0)
 
 
 def stencil(padded, width):

time: 341 us -> 546 us (1.60)
  waiting for transfers between devices: 179 us -> 458 us
  blocking collectives: 103 us -> 26.3 us
    unnamed x3 -> x5, waiting for transfers between devices: 0.05 us -> 243 us
    psum x1 -> x0, blocking collectives: 77 us -> none  [energy_sum(): return lax.psum(energy_part, ('space', 'tm'))]
    reduce_scatter x1, waiting for transfers between devices: 0.01 us -> 29.4 us  [shards(): lax.psum_scatter(change_part, 'space', scatter_dimension=1, tiled=True)]
    reduce_scatter x1, waiting for transfers between devices: 20.7 us -> 27.5 us  [shards(): lax.psum_scatter(partial_value, 'space', scatter_dimension=1, tiled=True)]
  transfers between devices with their start and end apart: 5 -> 6, of which waited for: 3 -> 4; matrix products, arithmetic and copies ran while one was open for 1% -> 1% of each run, Pallas kernels for 0% -> 0%
where the time goes in v1:
time: 546 us; the launch traced here: 545 us
  waiting for transfers between devices  458 us (84%)
  matrix products  28.1 us (5%)
  blocking collectives  26.3 us (5%)
  between operations  14.6 us (3%)
  other arithmetic  9.04 us (2%)
    unnamed x5, waiting for transfers between devices  243 us
    psum x1, waiting for transfers between devices, shards(): gram_part, side_part = lax.psum((gram_part, side_part), 'tm')  158 us
    reduce_scatter x1, waiting for transfers between devices, shards(): lax.psum_scatter(change_part, 'space', scatter_dimension=1, tiled=True)  29.4 us
    reduce_scatter x1, waiting for transfers between devices, shards(): lax.psum_scatter(partial_value, 'space', scatter_dimension=1, tiled=True)  27.5 us
    all_gather x1, blocking collectives, shards(): lax.all_gather(masked, 'space', axis=1, tiled=True)  13.3 us
    all_gather x1, blocking collectives, shards(): lax.all_gather(dmasked, 'space', axis=1, tiled=True)  13 us
    dot_general x2, matrix products, outer_rows(): jnp.einsum('tf,tg->fg', left_part, right_part, precision=EXACT, preferred...  11.8 us
  transfers between devices with their start and end apart: 6, of which 4 were waited for; matrix products, arithmetic and copies ran while one was open for 1% of the time, Pallas kernels for 0%

profile of v1, /device:TPU:8, one launch (start us, length us, event | category | flops | bytes accessed | tf_op | source)
XLA Modules:
  0.0 545.3 jit_solution(5896335886816280176)
XLA Ops:
  7.2 1.5 copy-done
  8.8 2.1 fusion.14
  10.9 0.9 fusion.13
  11.8 3.8 collective-permute-start
  15.6 1.3 collective-permute-start.1
  17.1 27.5 %reduce-scatter.3.cloned.1.call-done = f32[64,128]{1,0:T(8,128)} async-done(((f32[64,1024]{1,0:T(8,128)}), f32[64,128]{1,0:T(8,128)}) %reduce-scatter.3.cloned.1.call-update) | async-done | bytes 32784 | tf_op jit(solution)/shard_map/reduce_scatter | solution.py:70
  44.5 0.9 multiply_reduce_fusion
  45.4 0.3 dynamic-update-slice
  45.7 0.6 copy-done.3
  46.4 2.4 fusion.7
  48.9 0.6 add_reduce_fusion
  50.2 242.9 %all-reduce.5.cloned.1.call-done = f32[16384]{0:T(1024)} async-done(((f32[16384]{0:T(1024)}), f32[16384]{0:T(1024)}) %all-reduce.5.cloned.1.call-update) | async-done | bytes 65552
  293.1 0.9 reshape.64
  294.1 29.4 %reduce-scatter.5.cloned.1.call-done = f32[64,128]{1,0:T(8,128)} async-done(((f32[64,1024]{1,0:T(8,128)}), f32[64,128]{1,0:T(8,128)}) %reduce-scatter.5.cloned.1.call-update) | async-done | bytes 32784 | tf_op jit(solution)/shard_map/reduce_scatter | solution.py:71
  323.5 0.9 multiply_divide_fusion
  324.3 13.3 %all_gather.14 = f32[64,1024]{1,0:T(8,128)S(1)} all-gather(f32[64,128]{1,0:T(8,128)S(1)} %get-tuple-element.7), channel_id=1, replica_groups=mesh['space'=8,'tm'=32] {'space'}, dimensions={1}, use_global_device_ids=true | all-gather | bytes 294912 | tf_op jit(solution)/shard_map/all_gather | solution.py:96
  337.6 7.0 %fusion.15 = f32[1024,2080]{0,1:T(8,128)S(1)} fusion(f32[64,1024]{1,0:T(8,128)S(1)} %all_gather.14, f32[64,2080]{1,0:T(8,128)S(1)} %copy-done.2), kind=kOutput, calls=%fused_computation.44 | convolution fusion | flops 1635778560 | bytes 9314304 | tf_op jit(solution)/shard_map/dot_general | solution.py:38
  344.6 7.3 %convolution_multiply_fusion = f32[1024,2080]{0,1:T(8,128)S(1)} fusion(f32[1024,2080]{0,1:T(8,128)S(1)} %fusion.15, f32[64,1024]{1,0:T(8,128)S(1)} %all_gather.14, f32[64,2080]{1,0:T(8,128)S(1)} %copy-done.1), kind=kOutput, calls=%fused_computation.5 | convolution fusion | flops 1637908480 | bytes 17833984 | tf_op jit(solution)/shard_map/dot_general | solution.py:39
  352.1 9.9 %fusion = f32[268,2144]{1,0:T(8,128)} fusion(f32[1024,268]{0,1:T(8,128)S(1)} %fusion.2, f32[1024,64]{0,1:T(8,128)S(1)} %bitcast.11, f32[1024,2080]{0,1:T(8,128)S(1)} %convolution_multiply_fusion), kind=kOutput, calls=%fused_computation.2 | convolution fusion | flops 7062781952 | bytes 12177920 | tf_op jit(solution)/shard_map/tf,tg->fg/dot_general | solution.py:44
  362.0 13.0 %all_gather.15 = f32[64,1024]{1,0:T(8,128)S(1)} all-gather(f32[64,128]{1,0:T(8,128)S(1)} %get-tuple-element.6), channel_id=1, replica_groups=mesh['space'=8,'tm'=32] {'space'}, dimensions={1}, use_global_device_ids=true | all-gather | bytes 294912 | tf_op jit(solution)/shard_map/all_gather | solution.py:97
  375.0 1.9 fusion.16
  376.9 157.9 %all-reduce.7.cloned.1.call-done = (f32[268,2144]{1,0:T(8,128)}, f32[268,64]{0,1:T(8,128)}) async-done(((f32[268,2144]{1,0:T(8,128)}, f32[268,64]{0,1:T(8,128)}), (f32[268,2144]{1,0:T(8,128)}, f32[268,64]{0,1:T(8,128)})) %all-reduce.7.cloned.1.call-update) | async-done | bytes 2366992 | tf_op jit(solution)/shard_map/psum | solution.py:103
  534.9 3.3 broadcast_divide_fusion
  538.1 0.7 broadcast_divide_fusion.1
  (27 shorter events, 0.7 us)
Async XLA Ops:
  7.2 1.6 copy-start
  7.2 330.4 %copy-start.2 = (f32[64,2080]{1,0:T(8,128)S(1)}, f32[64,2080]{1,0:T(8,128)}, u32[]{:S(2)}) copy-start(f32[64,2080]{1,0:T(8,128)} %constant.80.clone) | copy-start | bytes 1597444
  7.2 9.8 %copy-start.5 = (s32[16]{0:T(128)S(1)}, s32[16]{0:T(128)}, u32[]{:S(2)}) copy-start(s32[16]{0:T(128)} %param.7) | copy-start | bytes 196
  7.2 37.3 %reduce-scatter.3.cloned.1.call-start = ((), (), s32[]{:S(2)}) async-start(), calls=%async_computation.2 | async-start | bytes 294912 | tf_op jit(solution)/shard_map/reduce_scatter | solution.py:70
  10.9 282.2 %all-reduce.5.cloned.1.call-start = ((), (), s32[]{:S(2)}) async-start(), calls=%async_computation.4 | async-start | bytes 131072
  11.8 34.6 %collective-permute-start = (f32[64,2]{1,0:T(8,128)S(1)}, f32[64,2]{1,0:T(8,128)S(1)}, u32[]{:S(2)}, u32[]{:S(2)}) collective-permute-start(f32[64,2]{1,0:T(8,128)S(1)} %get-tuple-element.4), channel_id=1, source_target_pairs={{0,1},{1,2},{2,3},{3,4},{4,5},{5,6},{6,7},{7,8},{8,9},{9,10},{10,1... | collective-permute-start | bytes 1544 | tf_op jit(solution)/shard_map/ppermute | solution.py:19
  15.6 30.8 %collective-permute-start.1 = (f32[64,2]{1,0:T(8,128)S(1)}, f32[64,2]{1,0:T(8,128)S(1)}, u32[]{:S(2)}, u32[]{:S(2)}) collective-permute-start(f32[64,2]{1,0:T(8,128)S(1)} %get-tuple-element.5), channel_id=1, source_target_pairs={{1,0},{2,1},{3,2},{4,3},{5,4},{6,5},{7,6},{8,7},{9,8},{10,9},{11,1... | collective-permute-start | bytes 1544 | tf_op jit(solution)/shard_map/ppermute | solution.py:21
  45.7 0.6 copy-start.3
  46.4 277.1 %reduce-scatter.5.cloned.1.call-start = ((), (), s32[]{:S(2)}) async-start(), calls=%async_computation.3 | async-start | bytes 294912 | tf_op jit(solution)/shard_map/reduce_scatter | solution.py:71
  48.8 486.0 %all-reduce.7.cloned.1.call-start = ((), (), s32[]{:S(2)}) async-start(), calls=%async_computation.5 | async-start | bytes 4931584 | tf_op jit(solution)/shard_map/psum | solution.py:103
  337.6 7.0 %copy-start.1 = (f32[64,2080]{1,0:T(8,128)S(1)}, f32[64,2080]{1,0:T(8,128)}, u32[]{:S(2)}) copy-start(f32[64,2080]{1,0:T(8,128)} %constant.81.clone) | copy-start | bytes 1597444
  534.9 3.3 copy-start.4
Sparse Core Ops, SparseCore 0:
  11.1 33.4 reduce-scatter.2
  50.6 242.3 all-reduce.4
  295.6 27.8 reduce-scatter.4
  377.1 157.7 all-reduce.6
